TPU v7x, 32 devices: a whole 2x2x4 slice. The times are simulated.
32 devices in a mesh: ctx: 8 (over z, x), head: 4 (over y, core).
Axes of the slice: x: 2, y: 2, z: 4, core: 2. Of those that a mesh axis runs over, the one named last changes fastest.
Arguments:
- queries: bfloat16 [1024, 4096], P('ctx', 'head'), may hold values from -24 to 24
- key_rows: bfloat16 [1024, 4096], P('ctx', 'head'), may hold values from -24 to 24
- value_rows: bfloat16 [1024, 4096], P('ctx', 'head'), may hold values from -6 to 6
- upstream: bfloat16 [1024, 6144], P('ctx', 'head'), may hold values from -6 to 6
- out_weight: bfloat16 [6144, 4096], P('ctx', 'head'), may hold values from -0.078125 to 0.078125
- group_ids: int32 [1024], replicated, may hold values from 0 to 7, never falling along the last dimension, each value on 1 to 256 neighbouring positions
Outputs:
- grad_queries: bfloat16 [1024, 4096], P('ctx', 'head')
- grad_keys: bfloat16 [1024, 4096], P('ctx', 'head')
- grad_values: bfloat16 [1024, 4096], P('ctx', 'head')
Inputs may be any that keep to these rules, and one draw needn't show every extreme that they name: `group_ids`: never falling along the tokens; each group number covers 1 to 256 consecutive tokens, one exactly 256.
All inputs are finite; a program needn't handle non-finite values.
Results may differ from a plain program's by a relative error of at most 0.025.
Values may be sent and summed in bfloat16 or wider, within the bound.
No kernel may reach another device: no remote copies, remote signals or barrier semaphores. Data moves between devices by JAX's collectives and lax.ppermute only.
A program may use at most 64 MiB of HBM per device.

v0:
```python
import jax
import jax.numpy as jnp
from jax import lax
from jax.sharding import PartitionSpec as P

HDIM = 128
masked_score = -1e30


def body(queries, key_rows, value_rows, upstream, out_weight, group_ids):
    rows_dev = queries.shape[0]
    heads_dev = queries.shape[1] // HDIM
    scaling = HDIM ** (-0.5)
    own_start = lax.axis_index("ctx") * rows_dev
    own_ids = lax.dynamic_slice_in_dim(group_ids, own_start, rows_dev, 0)
    upstream_full = lax.all_gather(upstream, "head", axis=1, tiled=True)
    grad_out = jnp.dot(
        upstream_full,
        lax.all_gather(out_weight, "ctx", axis=0, tiled=True),
        preferred_element_type=jnp.float32,
    ).astype(jnp.bfloat16)
    query_heads = queries.reshape(rows_dev, heads_dev, HDIM)
    grad_heads = grad_out.reshape(rows_dev, heads_dev, HDIM)
    key_heads = key_rows.reshape(rows_dev, heads_dev, HDIM)
    value_heads = value_rows.reshape(rows_dev, heads_dev, HDIM)
    stats_shape = (heads_dev, rows_dev)
    key_piece = lax.all_gather(key_rows, "ctx", axis=0, tiled=True)
    piece_rows = key_piece.shape[0]
    piece_ids = group_ids
    key_block = key_piece.reshape(piece_rows, heads_dev, HDIM)
    allowed = (piece_ids[None, :] <= own_ids[:, None])[None]
    run_max = jnp.full(stats_shape, masked_score, jnp.float32)
    scores = scaling * jnp.einsum(
        "qhd,khd->hqk", query_heads, key_block, preferred_element_type=jnp.float32
    )
    scores = jnp.where(allowed, scores, masked_score)
    new_max = jnp.maximum(run_max, jnp.max(scores, axis=2))
    weights = jnp.where(allowed, jnp.exp(scores - new_max[:, :, None]), 0.0)
    run_sum = jnp.sum(weights, axis=2)
    run_max, run_sum = (new_max, run_sum)
    log_total = run_max + jnp.log(run_sum)
    key_piece = lax.all_gather(key_rows, "ctx", axis=0, tiled=True)
    value_piece = lax.all_gather(value_rows, "ctx", axis=0, tiled=True)
    piece_rows = key_piece.shape[0]
    piece_ids = group_ids
    key_block = key_piece.reshape(piece_rows, heads_dev, HDIM)
    value_block = value_piece.reshape(piece_rows, heads_dev, HDIM)
    allowed = (piece_ids[None, :] <= own_ids[:, None])[None]
    scores = scaling * jnp.einsum(
        "qhd,khd->hqk", query_heads, key_block, preferred_element_type=jnp.float32
    )
    probs = jnp.where(allowed, jnp.exp(scores - log_total[:, :, None]), 0.0)
    probs_low = probs.astype(jnp.bfloat16)
    grad_probs = jnp.einsum(
        "qhd,khd->hqk", grad_heads, value_block, preferred_element_type=jnp.float32
    )
    mixed_low = (probs * grad_probs).astype(jnp.bfloat16)
    out_acc = jnp.einsum("hqk,khd->hqd", probs_low, value_block, preferred_element_type=jnp.float32)
    mixed_acc = jnp.einsum("hqk,khd->hqd", mixed_low, key_block, preferred_element_type=jnp.float32)
    plain_acc = jnp.einsum("hqk,khd->hqd", probs_low, key_block, preferred_element_type=jnp.float32)
    forward = (out_acc, mixed_acc, plain_acc)
    attn_out, mixed_acc, plain_acc = forward
    delta = jnp.einsum("qhd,hqd->hq", grad_heads.astype(jnp.float32), attn_out)
    grad_query = scaling * (mixed_acc - delta[:, :, None] * plain_acc)
    grad_queries = (
        grad_query.transpose(1, 0, 2).reshape(rows_dev, heads_dev * HDIM).astype(jnp.bfloat16)
    )
    all_lse, all_delta = (
        lax.all_gather(log_total.T, "ctx", axis=0, tiled=True),
        lax.all_gather(delta.T, "ctx", axis=0, tiled=True),
    )
    query_piece = lax.all_gather(queries, "ctx", axis=0, tiled=True)
    grad_piece = lax.all_gather(grad_out, "ctx", axis=0, tiled=True)
    piece_rows = query_piece.shape[0]
    piece_ids = group_ids
    piece_lse = all_lse.T
    piece_delta = all_delta.T
    query_block = query_piece.reshape(piece_rows, heads_dev, HDIM)
    grad_block = grad_piece.reshape(piece_rows, heads_dev, HDIM)
    allowed = (own_ids[None, :] <= piece_ids[:, None])[None]
    scores = scaling * jnp.einsum(
        "qhd,khd->hqk", query_block, key_heads, preferred_element_type=jnp.float32
    )
    probs = jnp.where(allowed, jnp.exp(scores - piece_lse[:, :, None]), 0.0)
    probs_low = probs.astype(jnp.bfloat16)
    grad_probs = jnp.einsum(
        "qhd,khd->hqk", grad_block, value_heads, preferred_element_type=jnp.float32
    )
    grad_scores = (probs * (grad_probs - piece_delta[:, :, None])).astype(jnp.bfloat16)
    value_grad = jnp.einsum(
        "hqk,qhd->hkd", probs_low, grad_block, preferred_element_type=jnp.float32
    )
    key_grad = jnp.einsum(
        "hqk,qhd->hkd", grad_scores, query_block, preferred_element_type=jnp.float32
    )
    key_grad, value_grad = (key_grad, value_grad)
    grad_keys = (
        (scaling * key_grad)
        .transpose(1, 0, 2)
        .reshape(rows_dev, heads_dev * HDIM)
        .astype(jnp.bfloat16)
    )
    grad_values = (
        value_grad.transpose(1, 0, 2).reshape(rows_dev, heads_dev * HDIM).astype(jnp.bfloat16)
    )
    return (grad_queries, grad_keys, grad_values)


def solution(mesh):
    in_specs = (
        P("ctx", "head"),
        P("ctx", "head"),
        P("ctx", "head"),
        P("ctx", "head"),
        P("ctx", "head"),
        P(),
    )
    out_specs = (P("ctx", "head"), P("ctx", "head"), P("ctx", "head"))
    return jax.shard_map(body, mesh=mesh, in_specs=in_specs, out_specs=out_specs, check_vma=False)
```

profile of v0, /device:TPU:0, one launch (start us, length us, event | category | flops | bytes accessed | tf_op | source)
XLA Modules:
  0.0 434.6 jit_solution(9773748842374155028)
XLA Ops:
  7.2 0.7 all-gather.9.cloned.1.call-update
  8.0 0.7 all-gather.11.cloned.1.call-update
  8.7 1.8 copy.18
  10.6 1.8 copy.21
  12.4 0.5 all-gather.13.cloned.1.call-update
  13.0 1.1 copy.41
  14.2 0.1 dynamic_slice.3
  14.2 0.1 broadcast_compare_fusion.1
  14.4 17.5 %all-gather.9.cloned.1.call-done = bf16[128,6144]{1,0:T(8,128)(2,1)} async-done(((bf16[128,1536]{1,0:T(8,128)(2,1)}), bf16[128,6144]{1,0:T(8,128)(2,1)}) %all-gather.9.cloned.1.call-update) | async-done | bytes 1572880 | tf_op jit(solution)/shard_map/all_gather | solution.py:16
  31.9 178.3 %all-gather.11.cloned.1.call-done = bf16[6144,1024]{1,0:T(8,128)(2,1)} async-done(((bf16[768,1024]{1,0:T(8,128)(2,1)}), bf16[6144,1024]{1,0:T(8,128)(2,1)}) %all-gather.11.cloned.1.call-update) | async-done | bytes 12582928 | tf_op jit(solution)/shard_map/all_gather | solution.py:19
  210.2 7.6 %convolution_convert_fusion = bf16[128,1024]{1,0:T(8,128)(2,1)} fusion(bf16[128,6144]{1,0:T(8,128)(2,1)} %all-gather.9.cloned.1.call-done, bf16[6144,1024]{1,0:T(8,128)(2,1)} %all-gather.11.cloned.1.call-done), kind=kOutput, calls=%fused_computation.28 | convolution fusion | flops 1610743808 | bytes 14417920 | tf_op jit(solution)/shard_map/dot_general | solution.py:17
  217.8 0.2 broadcast_compare_fusion
  218.0 43.4 %all-gather.7.cloned.1.call-done = bf16[1024,1024]{0,1:T(8,128)(2,1)} async-done(((bf16[128,1024]{0,1:T(8,128)(2,1)}), bf16[1024,1024]{0,1:T(8,128)(2,1)}) %all-gather.7.cloned.1.call-update) | async-done | bytes 2097168 | tf_op jit(solution)/shard_map/all_gather | solution.py:42
  261.4 2.7 select_reduce_fusion.1
  264.2 2.0 copy-done
  266.2 1.3 select_reduce_fusion
  267.5 31.1 %all_gather.30 = f32[1024,8]{0,1:T(8,128)S(1)} all-gather(f32[128,8]{0,1:T(8,128)S(1)} %bitcast.100), channel_id=1, replica_groups=mesh['ctx'=8,'head'=4] {'ctx'}, dimensions={0}, use_global_device_ids=true | all-gather | bytes 36864 | tf_op jit(solution)/shard_map/all_gather | solution.py:69
  298.6 13.9 %all-gather.15.cloned.1.call-done = bf16[1024,1024]{0,1:T(8,128)(2,1)} async-done(((bf16[128,1024]{0,1:T(8,128)(2,1)}), bf16[1024,1024]{0,1:T(8,128)(2,1)}) %all-gather.15.cloned.1.call-update) | async-done | bytes 2097168 | tf_op jit(solution)/shard_map/all_gather | solution.py:72
  312.5 4.4 %fusion.32 = f32[8,1024,128]{2,1,0:T(8,128)} fusion(bf16[1024,8,128]{0,2,1:T(8,128)(2,1)} %bitcast.85, bf16[128,1024]{1,0:T(8,128)(2,1)S(1)} %copy-done.5), kind=kOutput, calls=%fused_computation.32 | convolution fusion | flops 268435456 | bytes 6553600 | tf_op jit(solution)/shard_map/qhd,khd->hqk/dot_general | solution.py:81
  316.8 44.9 %all-gather.13.cloned.1.call-done = bf16[1024,1024]{1,0:T(8,128)(2,1)} async-done(((bf16[128,1024]{1,0:T(8,128)(2,1)}), bf16[1024,1024]{1,0:T(8,128)(2,1)}) %all-gather.13.cloned.1.call-update) | async-done | bytes 2097168 | tf_op jit(solution)/shard_map/all_gather | solution.py:43
  361.7 4.1 fusion.17
  365.9 0.4 multiply_reduce_fusion
  366.4 5.0 %fusion.20 = f32[128,8,128]{0,2,1:T(8,128)S(1)} fusion(bf16[1024,8,128]{0,2,1:T(8,128)(2,1)S(1)} %bitcast.88, f32[8,128,1024]{2,1,0:T(8,128)} %copy-done, f32[8,128]{1,0:T(8,128)S(1)} %log_add_fusion, pred[128,1024]{1,0:T(8,128)(4,1)S(1)} %broadcast_compare_fusion.1, bf16[1024,1024]{1,0:T(8,128)(2,1)} %all-gather.13.cloned.1.call-done, ...), kind=kOutput, calls=%fused_computation.22 | convolution fusion | flops 542113792 | bytes 9310208 | tf_op jit(solution)/shard_map/hqk,khd->hqd/dot_general | solution.py:59
  371.4 3.4 fusion.28
  374.8 0.9 copy.25
  375.6 31.3 %all_gather.32 = f32[1024,8]{0,1:T(8,128)S(1)} all-gather(f32[128,8]{0,1:T(8,128)S(1)} %copy.37), channel_id=1, replica_groups=mesh['ctx'=8,'head'=4] {'ctx'}, dimensions={0}, use_global_device_ids=true | all-gather | bytes 36864 | tf_op jit(solution)/shard_map/all_gather | solution.py:70
  406.9 5.4 %all-gather.17.cloned.1.call-done = bf16[1024,1024]{1,0:T(8,128)(2,1)} async-done(((bf16[128,1024]{1,0:T(8,128)(2,1)}), bf16[1024,1024]{1,0:T(8,128)(2,1)}) %all-gather.17.cloned.1.call-update) | async-done | bytes 2097168 | tf_op jit(solution)/shard_map/all_gather | solution.py:73
  412.4 3.9 copy.42
  416.3 3.9 fusion.29
  420.2 0.9 copy.27
  421.0 5.9 %fusion.27 = bf16[8,128,128]{1,2,0:T(8,128)(2,1)S(1)} fusion(bf16[1024,8,128]{0,2,1:T(8,128)(2,1)S(1)} %bitcast.86, f32[8,1024,128]{2,1,0:T(8,128)} %fusion.32, bf16[1024,8,128]{0,2,1:T(8,128)(2,1)} %bitcast.91, bf16[128,8,128]{0,2,1:T(8,128)(2,1)S(1)} %bitcast.93, f32[8,1024]{1,0:T(8,128)S(1)} %bitcast.99, f32[8,1024]{1,0:T(8,128)S(1)} %bitcast.98, ...), kind=kOutput, calls=%fused_computation.27 | convolution fusion | flops 543424512 | bytes 9109504 | tf_op jit(solution)/shard_map/hqk,qhd->hkd/dot_general | solution.py:93
  426.9 0.9 copy.26
  (26 shorter events, 0.4 us)
Async XLA Ops:
  7.2 7.0 %copy-start.6 = (s32[1024]{0:T(1024)S(1)}, s32[1024]{0:T(1024)}, u32[]{:S(2)}) copy-start(s32[1024]{0:T(1024)} %param.11) | copy-start | bytes 12292
  7.2 24.8 %all-gather.9.cloned.1.call-start = ((), (), s32[]{:S(2)}) async-start(), calls=%async_computation.1 | async-start | bytes 1966080 | tf_op jit(solution)/shard_map/all_gather | solution.py:16
  7.9 202.3 %all-gather.11.cloned.1.call-start = ((), (), s32[]{:S(2)}) async-start(), calls=%async_computation.2 | async-start | bytes 14155776 | tf_op jit(solution)/shard_map/all_gather | solution.py:19
  8.7 252.8 %all-gather.7.cloned.1.call-start = ((), (), s32[]{:S(2)}) async-start(), calls=%async_computation | async-start | bytes 2359296 | tf_op jit(solution)/shard_map/all_gather | solution.py:42
  10.5 301.9 %all-gather.15.cloned.1.call-start = ((), (), s32[]{:S(2)}) async-start(), calls=%async_computation.4 | async-start | bytes 2359296 | tf_op jit(solution)/shard_map/all_gather | solution.py:72
  12.4 349.4 %all-gather.13.cloned.1.call-start = ((), (), s32[]{:S(2)}) async-start(), calls=%async_computation.3 | async-start | bytes 2359296 | tf_op jit(solution)/shard_map/all_gather | solution.py:43
  13.0 399.4 %all-gather.17.cloned.1.call-start = ((), (), s32[]{:S(2)}) async-start(), calls=%async_computation.5 | async-start | bytes 2359296 | tf_op jit(solution)/shard_map/all_gather | solution.py:73
  14.4 247.0 %copy-start.4 = (bf16[128,1024]{1,0:T(8,128)(2,1)S(1)}, bf16[128,1024]{1,0:T(8,128)(2,1)}, u32[]{:S(2)}) copy-start(bf16[128,1024]{1,0:T(8,128)(2,1)} %param.6) | copy-start | bytes 786436
  261.4 51.0 %copy-start.5 = (bf16[128,1024]{1,0:T(8,128)(2,1)S(1)}, bf16[128,1024]{1,0:T(8,128)(2,1)}, u32[]{:S(2)}) copy-start(bf16[128,1024]{1,0:T(8,128)(2,1)} %param.7) | copy-start | bytes 786436
  264.2 2.0 copy-start
  316.8 49.0 %copy-start.1 = (bf16[128,1024]{1,0:T(8,128)(2,1)S(1)}, bf16[128,1024]{1,0:T(8,128)(2,1)}, u32[]{:S(2)}) copy-start(bf16[128,1024]{1,0:T(8,128)(2,1)} %convolution_convert_fusion) | copy-start | bytes 786436
  316.8 49.5 %copy-start.3 = (bf16[1024,1024]{0,1:T(8,128)(2,1)S(1)}, bf16[1024,1024]{0,1:T(8,128)(2,1)}, u32[]{:S(2)}) copy-start(bf16[1024,1024]{0,1:T(8,128)(2,1)} %all-gather.7.cloned.1.call-done) | copy-start | bytes 6291460
  416.3 4.7 %copy-start.2 = (bf16[1024,1024]{0,1:T(8,128)(2,1)S(1)}, bf16[1024,1024]{0,1:T(8,128)(2,1)}, u32[]{:S(2)}) copy-start(bf16[1024,1024]{0,1:T(8,128)(2,1)} %all-gather.15.cloned.1.call-done) | copy-start | bytes 6291460
Sparse Core Ops, SparseCore 0:
  9.5 22.3 all-gather.8
  34.1 176.0 all-gather.10
  212.9 48.5 all-gather.6
  263.9 48.4 all-gather.14
  314.4 47.2 all-gather.12
  364.3 48.0 all-gather.16
where the time goes:
time: 435 us
  waiting for transfers between devices  305 us (70%)
  blocking collectives  62.4 us (14%)
  matrix products  36.9 us (8%)
  between operations  14.2 us (3%)
  local copies, waits for them, and re-layouts  13.3 us (3%)
    all_gather x1, waiting for transfers between devices, body(): lax.all_gather(out_weight, 'ctx', axis=0, tiled=True)  178 us
    all_gather x1, waiting for transfers between devices, body(): value_piece = lax.all_gather(value_rows, 'ctx', axis=0, tiled=True)  44.9 us
    all_gather x1, waiting for transfers between devices, body(): key_piece = lax.all_gather(key_rows, 'ctx', axis=0, tiled=True)  43.4 us
    all_gather x1, blocking collectives, body(): lax.all_gather(delta.T, 'ctx', axis=0, tiled=True)  31.3 us
    all_gather x1, blocking collectives, body(): lax.all_gather(log_total.T, 'ctx', axis=0, tiled=True)  31.1 us
    all_gather x1, waiting for transfers between devices, body(): upstream_full = lax.all_gather(upstream, 'head', axis=1, tiled=True)  17.5 us
    all_gather x1, waiting for transfers between devices, body(): query_piece = lax.all_gather(queries, 'ctx', axis=0, tiled=True)  13.9 us
  transfers between devices with their start and end apart: 6, of which 6 were waited for; matrix products, arithmetic and copies ran while one was open for 8% of the time, Pallas kernels for 0%

commit v1 on v0

--- a/solution.py
+++ b/solution.py
@@ -66,7 +66,9 @@
         grad_query.transpose(1, 0, 2).reshape(rows_dev, heads_dev * HDIM).astype(jnp.bfloat16)
     )
     all_lse, all_delta = (
-        lax.all_gather(log_total.T, "ctx", axis=0, tiled=True),
+        jnp.concatenate(
+            lax.all_to_all(jnp.stack([log_total.T] * lax.axis_size("ctx")), "ctx", 0, 0), axis=0
+        ),
         lax.all_gather(delta.T, "ctx", axis=0, tiled=True),
     )
     query_piece = lax.all_gather(queries, "ctx", axis=0, tiled=True)

time: 435 us -> 436 us (level)
  blocking collectives: 62.4 us -> 31.3 us
  waiting for transfers between devices: 305 us -> 333 us
    all_gather x1 -> x0, blocking collectives: 31.1 us -> none  [body(): lax.all_gather(log_total.T, 'ctx', axis=0, tiled=True)]
    all_gather x1, waiting for transfers between devices: 13.9 us -> 41.4 us  [body(): query_piece = lax.all_gather(queries, 'ctx', axis=0, tiled=True)]
  transfers between devices with their start and end apart: 6 -> 7, of which waited for: 6 -> 6; matrix products, arithmetic and copies ran while one was open for 8% -> 9% of each run, Pallas kernels for 0% -> 0%
where the time goes in v1:
time: 436 us; the launch traced here: 435 us
  waiting for transfers between devices  333 us (76%)
  matrix products  36.9 us (8%)
  blocking collectives  31.3 us (7%)
  between operations  14.2 us (3%)
  local copies, waits for them, and re-layouts  14 us (3%)
    all_gather x1, waiting for transfers between devices, body(): lax.all_gather(out_weight, 'ctx', axis=0, tiled=True)  178 us
    all_gather x1, waiting for transfers between devices, body(): value_piece = lax.all_gather(value_rows, 'ctx', axis=0, tiled=True)  44.9 us
    all_gather x1, waiting for transfers between devices, body(): key_piece = lax.all_gather(key_rows, 'ctx', axis=0, tiled=True)  43.4 us
    all_gather x1, waiting for transfers between devices, body(): query_piece = lax.all_gather(queries, 'ctx', axis=0, tiled=True)  41.4 us
    all_gather x1, blocking collectives, body(): lax.all_gather(delta.T, 'ctx', axis=0, tiled=True)  31.3 us
    all_gather x1, waiting for transfers between devices, body(): upstream_full = lax.all_gather(upstream, 'head', axis=1, tiled=True)  17.5 us
  transfers between devices with their start and end apart: 7, of which 6 were waited for; matrix products, arithmetic and copies ran while one was open for 9% of the time, Pallas kernels for 0%

profile of v1, /device:TPU:0, one launch (start us, length us, event | category | flops | bytes accessed | tf_op | source)
XLA Modules:
  0.0 435.0 jit_solution(3788681493488493403)
XLA Ops:
  7.2 0.7 all-gather.9.cloned.1.call-update
  8.0 0.7 all-gather.11.cloned.1.call-update
  8.7 1.8 copy.18
  10.6 1.8 copy.21
  12.4 0.5 all-gather.13.cloned.1.call-update
  13.0 1.1 copy.41
  14.2 0.1 broadcast_compare_fusion.1
  14.4 17.5 %all-gather.9.cloned.1.call-done = bf16[128,6144]{1,0:T(8,128)(2,1)} async-done(((bf16[128,1536]{1,0:T(8,128)(2,1)}), bf16[128,6144]{1,0:T(8,128)(2,1)}) %all-gather.9.cloned.1.call-update) | async-done | bytes 1572880 | tf_op jit(solution)/shard_map/all_gather | solution.py:16
  31.9 178.3 %all-gather.11.cloned.1.call-done = bf16[6144,1024]{1,0:T(8,128)(2,1)} async-done(((bf16[768,1024]{1,0:T(8,128)(2,1)}), bf16[6144,1024]{1,0:T(8,128)(2,1)}) %all-gather.11.cloned.1.call-update) | async-done | bytes 12582928 | tf_op jit(solution)/shard_map/all_gather | solution.py:19
  210.2 7.6 %convolution_convert_fusion = bf16[128,1024]{1,0:T(8,128)(2,1)} fusion(bf16[128,6144]{1,0:T(8,128)(2,1)} %all-gather.9.cloned.1.call-done, bf16[6144,1024]{1,0:T(8,128)(2,1)} %all-gather.11.cloned.1.call-done), kind=kOutput, calls=%fused_computation.28 | convolution fusion | flops 1610743808 | bytes 14417920 | tf_op jit(solution)/shard_map/dot_general | solution.py:17
  217.8 0.2 broadcast_compare_fusion
  218.0 43.4 %all-gather.7.cloned.1.call-done = bf16[1024,1024]{0,1:T(8,128)(2,1)} async-done(((bf16[128,1024]{0,1:T(8,128)(2,1)}), bf16[1024,1024]{0,1:T(8,128)(2,1)}) %all-gather.7.cloned.1.call-update) | async-done | bytes 2097168 | tf_op jit(solution)/shard_map/all_gather | solution.py:42
  261.4 2.7 select_reduce_fusion.1
  264.2 2.0 copy-done
  266.2 1.3 select_reduce_fusion
  267.5 0.6 stack.2
  268.1 3.3 all-to-all-start
  271.5 41.4 %all-gather.15.cloned.1.call-done = bf16[1024,1024]{0,1:T(8,128)(2,1)} async-done(((bf16[128,1024]{0,1:T(8,128)(2,1)}), bf16[1024,1024]{0,1:T(8,128)(2,1)}) %all-gather.15.cloned.1.call-update) | async-done | bytes 2097168 | tf_op jit(solution)/shard_map/all_gather | solution.py:74
  312.9 4.4 %fusion.32 = f32[8,1024,128]{2,1,0:T(8,128)} fusion(bf16[1024,8,128]{0,2,1:T(8,128)(2,1)} %bitcast.87, bf16[128,1024]{1,0:T(8,128)(2,1)S(1)} %copy-done.5), kind=kOutput, calls=%fused_computation.32 | convolution fusion | flops 268435456 | bytes 6553600 | tf_op jit(solution)/shard_map/qhd,khd->hqk/dot_general | solution.py:83
  317.2 44.9 %all-gather.13.cloned.1.call-done = bf16[1024,1024]{1,0:T(8,128)(2,1)} async-done(((bf16[128,1024]{1,0:T(8,128)(2,1)}), bf16[1024,1024]{1,0:T(8,128)(2,1)}) %all-gather.13.cloned.1.call-update) | async-done | bytes 2097168 | tf_op jit(solution)/shard_map/all_gather | solution.py:43
  362.2 4.1 fusion.17
  366.3 0.4 multiply_reduce_fusion
  366.8 5.0 %fusion.20 = f32[128,8,128]{0,2,1:T(8,128)S(1)} fusion(bf16[1024,8,128]{0,2,1:T(8,128)(2,1)S(1)} %bitcast.90, f32[8,128,1024]{2,1,0:T(8,128)} %copy-done, f32[8,128]{1,0:T(8,128)S(1)} %log_add_fusion, pred[128,1024]{1,0:T(8,128)(4,1)S(1)} %broadcast_compare_fusion.1, bf16[1024,1024]{1,0:T(8,128)(2,1)} %all-gather.13.cloned.1.call-done, ...), kind=kOutput, calls=%fused_computation.22 | convolution fusion | flops 542113792 | bytes 9310208 | tf_op jit(solution)/shard_map/hqk,khd->hqd/dot_general | solution.py:59
  371.8 3.4 fusion.28
  375.2 0.9 copy.25
  376.0 31.3 %all_gather.28 = f32[1024,8]{0,1:T(8,128)S(1)} all-gather(f32[128,8]{0,1:T(8,128)S(1)} %copy.37), channel_id=1, replica_groups=mesh['ctx'=8,'head'=4] {'ctx'}, dimensions={0}, use_global_device_ids=true | all-gather | bytes 36864 | tf_op jit(solution)/shard_map/all_gather | solution.py:72
  407.3 5.4 %all-gather.17.cloned.1.call-done = bf16[1024,1024]{1,0:T(8,128)(2,1)} async-done(((bf16[128,1024]{1,0:T(8,128)(2,1)}), bf16[1024,1024]{1,0:T(8,128)(2,1)}) %all-gather.17.cloned.1.call-update) | async-done | bytes 2097168 | tf_op jit(solution)/shard_map/all_gather | solution.py:75
  412.8 3.9 copy.42
  416.7 3.9 fusion.29
  420.6 0.9 copy.27
  421.4 5.9 %fusion.27 = bf16[8,128,128]{1,2,0:T(8,128)(2,1)S(1)} fusion(bf16[1024,8,128]{0,2,1:T(8,128)(2,1)S(1)} %bitcast.88, f32[8,1024,128]{2,1,0:T(8,128)} %fusion.32, bf16[1024,8,128]{0,2,1:T(8,128)(2,1)} %bitcast.93, bf16[128,8,128]{0,2,1:T(8,128)(2,1)S(1)} %bitcast.95, f32[8,1024]{1,0:T(8,128)S(1)} %bitcast.99, f32[8,1024]{1,0:T(8,128)S(1)} %bitcast.101, ...), kind=kOutput, calls=%fused_computation.27 | convolution fusion | flops 543424512 | bytes 9109504 | tf_op jit(solution)/shard_map/hqk,qhd->hkd/dot_general | solution.py:95
  427.3 0.9 copy.26
  (28 shorter events, 0.5 us)
Async XLA Ops:
  7.2 7.0 %copy-start.6 = (s32[1024]{0:T(1024)S(1)}, s32[1024]{0:T(1024)}, u32[]{:S(2)}) copy-start(s32[1024]{0:T(1024)} %param.11) | copy-start | bytes 12292
  7.2 24.8 %all-gather.9.cloned.1.call-start = ((), (), s32[]{:S(2)}) async-start(), calls=%async_computation.2 | async-start | bytes 1966080 | tf_op jit(solution)/shard_map/all_gather | solution.py:16
  7.9 202.3 %all-gather.11.cloned.1.call-start = ((), (), s32[]{:S(2)}) async-start(), calls=%async_computation.3 | async-start | bytes 14155776 | tf_op jit(solution)/shard_map/all_gather | solution.py:19
  8.7 252.8 %all-gather.7.cloned.1.call-start = ((), (), s32[]{:S(2)}) async-start(), calls=%async_computation.1 | async-start | bytes 2359296 | tf_op jit(solution)/shard_map/all_gather | solution.py:42
  10.5 302.4 %all-gather.15.cloned.1.call-start = ((), (), s32[]{:S(2)}) async-start(), calls=%async_computation.5 | async-start | bytes 2359296 | tf_op jit(solution)/shard_map/all_gather | solution.py:74
  12.4 349.8 %all-gather.13.cloned.1.call-start = ((), (), s32[]{:S(2)}) async-start(), calls=%async_computation.4 | async-start | bytes 2359296 | tf_op jit(solution)/shard_map/all_gather | solution.py:43
  13.0 399.8 %all-gather.17.cloned.1.call-start = ((), (), s32[]{:S(2)}) async-start(), calls=%async_computation.6 | async-start | bytes 2359296 | tf_op jit(solution)/shard_map/all_gather | solution.py:75
  14.4 247.0 %copy-start.4 = (bf16[128,1024]{1,0:T(8,128)(2,1)S(1)}, bf16[128,1024]{1,0:T(8,128)(2,1)}, u32[]{:S(2)}) copy-start(bf16[128,1024]{1,0:T(8,128)(2,1)} %param.6) | copy-start | bytes 786436
  261.4 51.4 %copy-start.5 = (bf16[128,1024]{1,0:T(8,128)(2,1)S(1)}, bf16[128,1024]{1,0:T(8,128)(2,1)}, u32[]{:S(2)}) copy-start(bf16[128,1024]{1,0:T(8,128)(2,1)} %param.7) | copy-start | bytes 786436
  264.2 2.0 copy-start
  268.1 148.6 %all-to-all-start = ((f32[8,128,8]{1,2,0:T(8,128)}), f32[8,128,8]{1,2,0:T(8,128)S(1)}, u32[]{:S(2)}, u32[]{:S(2)}) async-start(f32[8,128,8]{1,2,0:T(8,128)} %stack.2), calls=%async_computation | async-start | bytes 65536 | tf_op jit(solution)/shard_map/all_to_all | solution.py:70
  317.2 49.0 %copy-start.1 = (bf16[128,1024]{1,0:T(8,128)(2,1)S(1)}, bf16[128,1024]{1,0:T(8,128)(2,1)}, u32[]{:S(2)}) copy-start(bf16[128,1024]{1,0:T(8,128)(2,1)} %convolution_convert_fusion) | copy-start | bytes 786436
  317.2 49.5 %copy-start.3 = (bf16[1024,1024]{0,1:T(8,128)(2,1)S(1)}, bf16[1024,1024]{0,1:T(8,128)(2,1)}, u32[]{:S(2)}) copy-start(bf16[1024,1024]{0,1:T(8,128)(2,1)} %all-gather.7.cloned.1.call-done) | copy-start | bytes 6291460
  416.7 4.7 %copy-start.2 = (bf16[1024,1024]{0,1:T(8,128)(2,1)S(1)}, bf16[1024,1024]{0,1:T(8,128)(2,1)}, u32[]{:S(2)}) copy-start(bf16[1024,1024]{0,1:T(8,128)(2,1)} %all-gather.15.cloned.1.call-done) | copy-start | bytes 6291460
Sparse Core Ops, SparseCore 0:
  9.5 22.3 all-gather.8
  34.1 176.0 all-gather.10
  212.9 48.5 all-gather.6
  263.9 48.9 all-gather.14
  314.8 47.2 all-gather.12
  364.7 48.0 all-gather.16
